TPU v7x, 32 devices: a whole 2x2x4 slice. The times are simulated.
32 devices in a mesh: tok: 8 (over z, x), head: 4 (over y, core).
Axes of the slice: x: 2, y: 2, z: 4, core: 2. Of those that a mesh axis runs over, the one named last changes fastest.
Arguments:
- queries: bfloat16 [2048, 8192], P(('tok', 'head')), may hold values from -6 to 6
- keys: bfloat16 [2048, 1024], P(('tok', 'head')), may hold values from -6 to 6
- values: bfloat16 [2048, 1024], P(('tok', 'head')), may hold values from -6 to 6
- doc_ids: int32 [2048], replicated, may hold values from 0 to 2, never falling along the last dimension, each value on 1 to 1792 neighbouring positions
Outputs:
- attention: bfloat16 [2048, 8192], P('tok', 'head')
Inputs may be any that keep to these rules, and one draw needn't show every extreme that they name: doc_ids never falls along the tokens; each document holds 1 to 1792 tokens and some document holds exactly 1792.
All inputs are finite; a program needn't handle non-finite values.
Results may differ from a plain program's by a relative error of at most 0.0038.
Values may be sent and summed in bfloat16 or wider, within the bound.
A program may use at most 64 MiB of HBM per device.

v0:
```python
import jax
import jax.numpy as jnp
from jax import lax
from jax.sharding import PartitionSpec as P

QH = 64
KVH = 8
HD = 128
REACH = 7


def from_behind(array, axis, by):
    length = lax.axis_size(axis)
    pairs = [(i, i + by) for i in range(length) if 0 <= i + by < length]
    return lax.ppermute(array, axis, pairs)


def body(queries, keys, values, doc_ids):
    local_queries, local_keys, local_values = (
        lax.all_to_all(queries, "head", split_axis=1, concat_axis=0, tiled=True),
        lax.all_to_all(keys, "head", split_axis=1, concat_axis=0, tiled=True),
        lax.all_to_all(values, "head", split_axis=1, concat_axis=0, tiled=True),
    )
    shard_rows = local_queries.shape[0]
    head_count = local_keys.shape[1] // HD
    groups = QH // KVH
    scaling = HD ** (-0.5)
    query_heads = local_queries.reshape(shard_rows, head_count, groups, HD)
    shard_index = lax.axis_index("tok")
    padded_ids = jnp.concatenate([jnp.full((REACH * shard_rows,), -1, jnp.int32), doc_ids], axis=0)
    own_ids = lax.dynamic_slice_in_dim(
        padded_ids, (shard_index + REACH) * shard_rows, shard_rows, 0
    )
    causal = jnp.arange(shard_rows)[None, :] <= jnp.arange(shard_rows)[:, None]

    def absorb(carry_state, key_pair, offset):
        key_ids = lax.dynamic_slice_in_dim(
            padded_ids, (shard_index + REACH - offset) * shard_rows, shard_rows, 0
        )
        visible = own_ids[:, None] == key_ids[None, :]
        if offset == 0:
            visible = visible & causal
        peak_now, weight_sum, numerator = carry_state
        key_block = key_pair[0].reshape(shard_rows, head_count, HD)
        value_block = key_pair[1].reshape(shard_rows, head_count, HD)
        scores = (
            jnp.einsum("qcgd,kcd->qcgk", query_heads, key_block, preferred_element_type=jnp.float32)
            * scaling
        )
        scores = jnp.where(visible[:, None, None, :], scores, -jnp.inf)
        peak_new = jnp.maximum(peak_now, jnp.max(scores, axis=-1))
        rescale = jnp.exp(peak_now - peak_new)
        weights = jnp.exp(scores - peak_new[..., None])
        weight_sum = weight_sum * rescale + jnp.sum(weights, axis=-1)
        rounded = weights.astype(jnp.bfloat16)
        numerator = numerator * rescale[..., None] + jnp.einsum(
            "qcgk,kcd->qcgd", rounded, value_block, preferred_element_type=jnp.float32
        )
        return (peak_new, weight_sum, numerator)

    start_state = (
        jnp.full((shard_rows, head_count, groups), -jnp.inf, jnp.float32),
        jnp.zeros((shard_rows, head_count, groups), jnp.float32),
        jnp.zeros((shard_rows, head_count, groups, HD), jnp.float32),
    )
    own_pair = jnp.stack([local_keys, local_values], axis=0)
    carry_state = absorb(start_state, own_pair, 0)
    window = own_pair[None]
    for section_level in range(REACH.bit_length()):
        extent = window.shape[0]
        arrived = from_behind(window, "tok", extent)
        for position in range(extent):
            offset = 2 * extent - 1 - position
            carry_state = absorb(carry_state, arrived[position], offset)
        window = jnp.concatenate([arrived, window], axis=0)
    peak_now, weight_sum, numerator = carry_state
    result = numerator / weight_sum[..., None]
    return result.reshape(shard_rows, head_count * groups * HD).astype(jnp.bfloat16)


def solution(mesh):
    return jax.shard_map(
        body,
        mesh=mesh,
        in_specs=(
            P(("tok", "head"), None),
            P(("tok", "head"), None),
            P(("tok", "head"), None),
            P(),
        ),
        out_specs=P("tok", "head"),
        check_vma=False,
    )
```

profile of v0, /device:TPU:25, one launch (start us, length us, event | category | flops | bytes accessed | tf_op | source)
XLA Modules:
  0.0 129.8 jit_solution(17575146356472023909)
XLA Ops:
  0.0 1.6 %copy.234 = bf16[8,4,8,256]{3,2,0,1:T(8,128)(2,1)} copy(bf16[8,4,8,256]{3,2,1,0:T(8,128)(2,1)} %bitcast.264) | data formatting | bytes 262144 | tf_op jit(solution)/shard_map/all_to_all | solution.py:21
  1.6 4.0 %all-to-all-start = ((bf16[64,4,256]{2,0,1:T(8,128)(2,1)}), bf16[64,4,256]{2,0,1:T(8,128)(2,1)S(1)}, u32[]{:S(2)}, u32[]{:S(2)}) async-start(bf16[64,4,256]{2,0,1:T(8,128)(2,1)} %bitcast.233), calls=%async_computation | async-start | bytes 262144 | tf_op jit(solution)/shard_map/all_to_all | solution.py:21
  5.6 1.5 %copy.233 = bf16[8,4,8,256]{3,2,0,1:T(8,128)(2,1)} copy(bf16[8,4,8,256]{3,2,1,0:T(8,128)(2,1)} %bitcast.265) | data formatting | bytes 262144 | tf_op jit(solution)/shard_map/all_to_all | solution.py:22
  7.1 2.0 %all-to-all-done = bf16[64,4,256]{2,0,1:T(8,128)(2,1)S(1)} async-done(((bf16[64,4,256]{2,0,1:T(8,128)(2,1)}), bf16[64,4,256]{2,0,1:T(8,128)(2,1)S(1)}, u32[]{:S(2)}, u32[]{:S(2)}) %all-to-all-start) | async-done | bytes 131104 | tf_op jit(solution)/shard_map/all_to_all | solution.py:21
  9.1 4.3 %all-to-all-start.2 = ((bf16[64,4,256]{2,0,1:T(8,128)(2,1)}), bf16[64,4,256]{2,0,1:T(8,128)(2,1)S(1)}, u32[]{:S(2)}, u32[]{:S(2)}) async-start(bf16[64,4,256]{2,0,1:T(8,128)(2,1)} %bitcast.232), calls=%async_computation.2 | async-start | bytes 262144 | tf_op jit(solution)/shard_map/all_to_all | solution.py:22
  13.4 2.3 %copy.232 = bf16[8,4,8,2048]{3,2,0,1:T(8,128)(2,1)} copy(bf16[8,4,8,2048]{3,2,1,0:T(8,128)(2,1)} %bitcast.247) | data formatting | bytes 2097152 | tf_op jit(solution)/shard_map/all_to_all | solution.py:20
  15.8 1.3 all-to-all-done.2
  17.0 4.5 %all-to-all-start.1 = ((bf16[64,4,2048]{2,0,1:T(8,128)(2,1)}), bf16[64,4,2048]{2,0,1:T(8,128)(2,1)S(1)}, u32[]{:S(2)}, u32[]{:S(2)}) async-start(bf16[64,4,2048]{2,0,1:T(8,128)(2,1)} %bitcast.231), calls=%async_computation.1 | async-start | bytes 2097152 | tf_op jit(solution)/shard_map/all_to_all | solution.py:20
  21.6 3.1 %collective-permute-start = (bf16[1,2,256,256]{3,2,1,0:T(8,128)(2,1)S(1)}, bf16[1,2,256,256]{3,2,1,0:T(8,128)(2,1)S(1)}, u32[]{:S(2)}, u32[]{:S(2)}) collective-permute-start(bf16[1,2,256,256]{3,2,1,0:T(8,128)(2,1)S(1)} %maximum_bitcast_fusion), channel_id=1, source_target_pairs={{0,4},{4,8},{8,12},{12,16},{16,20},{20,24},{24,28},{1,5},{5,9},{9,... | collective-permute-start | bytes 786440 | tf_op jit(solution)/shard_map/ppermute | solution.py:15
  24.7 0.0 copy-done.13
  24.7 0.1 pad_dynamic-slice_fusion.6
  24.8 1.0 broadcast_compare_fusion.6
  25.9 0.7 reshape_squeeze_stack.6
  26.6 0.7 reshape_squeeze_stack.7
  27.3 4.9 %collective-permute-done = bf16[1,2,256,256]{3,2,1,0:T(8,128)(2,1)S(1)} collective-permute-done((bf16[1,2,256,256]{3,2,1,0:T(8,128)(2,1)S(1)}, bf16[1,2,256,256]{3,2,1,0:T(8,128)(2,1)S(1)}, u32[]{:S(2)}, u32[]{:S(2)}) %collective-permute-start) | collective-permute-done | bytes 262176 | tf_op jit(solution)/shard_map/ppermute | solution.py:15
  32.2 0.7 copy.112
  33.0 0.8 copy.109
  33.7 0.8 pad_maximum_fusion.1
  34.5 1.3 collective-permute-start.1
  35.8 0.0 all-to-all-done.1
  35.8 0.2 copy.190
  36.1 1.8 %fusion.16 = (f32[256,2,8]{0,2,1:T(8,128)S(1)}, f32[2,256,256,8]{2,1,3,0:T(8,128)S(1)}) fusion(pred[256,256]{0,1:T(8,128)(4,1)S(1)} %get-tuple-element.50, bf16[256,2,8,128]{3,2,1,0:T(8,128)(2,1)S(1)} %bitcast.234, bf16[256,2,128,1]{2,1,0,3:T(2,128)(2,1)} %bitcast.258), kind=kOutput, calls=%fused_computation.32 | convolution fusion | flops 271577088 | bytes 5455872 | tf_op jit(solution)/shard_map/qcgd,kcd->qcgk/dot_general | solution.py:47
  37.9 0.0 copy-start
  37.9 3.7 %fusion.38 = f32[2,256,8,128]{1,3,2,0:T(8,128)} fusion(f32[2,256,256,8]{2,1,3,0:T(8,128)S(1)} %get-tuple-element.64, f32[256,2,8]{0,2,1:T(8,128)S(1)} %get-tuple-element.63, pred[256,256]{0,1:T(8,128)(4,1)S(1)} %get-tuple-element.50, bf16[256,2,128,1]{2,1,0,3:T(2,128)(2,1)} %bitcast.257), kind=kOutput, calls=%fused_computation.47 | convolution fusion | flops 272629760 | bytes 6504448 | tf_op jit(solution)/shard_map/qcgk,kcd->qcgd/dot_general | solution.py:56
  41.6 7.6 %collective-permute-done.1 = bf16[2,2,256,256]{3,2,1,0:T(8,128)(2,1)S(1)} collective-permute-done((bf16[2,2,256,256]{3,2,1,0:T(8,128)(2,1)}, bf16[2,2,256,256]{3,2,1,0:T(8,128)(2,1)S(1)}, u32[]{:S(2)}, u32[]{:S(2)}) %collective-permute-start.1) | collective-permute-done | bytes 524320 | tf_op jit(solution)/shard_map/ppermute | solution.py:15
  49.2 1.1 pad_maximum_fusion
  50.3 1.5 %collective-permute-start.2 = (bf16[4,2,256,256]{3,2,1,0:T(8,128)(2,1)}, bf16[4,2,256,256]{3,2,1,0:T(8,128)(2,1)S(1)}, u32[]{:S(2)}, u32[]{:S(2)}) collective-permute-start(bf16[4,2,256,256]{3,2,1,0:T(8,128)(2,1)} %pad_maximum_fusion), channel_id=1, source_target_pairs={{0,16},{4,20},{8,24},{12,28},{1,17},{5,21},{9,25},{13,29},{2,18},{... | collective-permute-start | bytes 3145736 | tf_op jit(solution)/shard_map/ppermute | solution.py:15
  51.8 3.5 %fusion.17 = (f32[256,2,8]{0,2,1:T(8,128)}, f32[2,256,256,8]{2,1,3,0:T(8,128)}) fusion(pred[256,256]{0,1:T(8,128)(4,1)S(1)} %get-tuple-element.43, bf16[256,2,128,1]{0,2,3,1:T(8,128)(2,1)S(1)} %bitcast.255, bf16[256,2,8,128]{3,2,1,0:T(8,128)(2,1)S(1)} %bitcast.235), kind=kOutput, calls=%fused_computation.33 | convolution fusion | flops 271577088 | bytes 5455872 | tf_op jit(solution)/shard_map/qcgd,kcd->qcgk/dot_general | solution.py:47
  55.3 0.7 fusion.120
  56.0 0.1 copy.117
  56.1 0.1 copy.122
  56.2 0.1 copy.119
  56.3 1.0 copy.114
  57.3 3.5 %fusion.18 = (f32[256,2,8]{0,2,1:T(8,128)}, f32[2,256,256,8]{2,1,3,0:T(8,128)}) fusion(pred[256,256]{0,1:T(8,128)(4,1)S(1)} %get-tuple-element.44, bf16[256,2,128,1]{0,2,3,1:T(8,128)(2,1)S(1)} %bitcast.262, bf16[256,2,8,128]{3,2,1,0:T(8,128)(2,1)S(1)} %bitcast.236), kind=kOutput, calls=%fused_computation.34 | convolution fusion | flops 271577088 | bytes 5455872 | tf_op jit(solution)/shard_map/qcgd,kcd->qcgk/dot_general | solution.py:47
  60.9 3.5 %fusion.19 = (f32[256,2,8]{0,2,1:T(8,128)}, f32[2,256,256,8]{2,1,3,0:T(8,128)}) fusion(pred[256,256]{0,1:T(8,128)(4,1)S(1)} %get-tuple-element.45, bf16[256,2,128,1]{0,2,3,1:T(8,128)(2,1)S(1)} %bitcast.261, bf16[256,2,8,128]{3,2,1,0:T(8,128)(2,1)S(1)} %bitcast.237), kind=kOutput, calls=%fused_computation.35 | convolution fusion | flops 271577088 | bytes 5455872 | tf_op jit(solution)/shard_map/qcgd,kcd->qcgk/dot_general | solution.py:47
  64.4 36.4 %collective-permute-done.2 = bf16[4,2,256,256]{3,2,1,0:T(8,128)(2,1)S(1)} collective-permute-done((bf16[4,2,256,256]{3,2,1,0:T(8,128)(2,1)}, bf16[4,2,256,256]{3,2,1,0:T(8,128)(2,1)S(1)}, u32[]{:S(2)}, u32[]{:S(2)}) %collective-permute-start.2) | collective-permute-done | bytes 1048608 | tf_op jit(solution)/shard_map/ppermute | solution.py:15
  100.7 0.8 fusion.119
  101.5 0.1 copy.142
  101.6 0.1 copy.139
  101.7 0.1 copy.137
  101.8 0.1 copy.134
  101.9 1.0 copy.132
  102.9 0.1 copy.129
  103.0 1.0 copy.127
  104.1 0.1 copy.124
  104.2 1.0 fusion.20
  105.2 1.0 fusion.21
  106.2 1.0 fusion.22
  107.2 1.0 fusion.23
  108.2 1.1 fusion.28
  109.4 2.0 %fusion.8 = (f32[256,2,8]{0,2,1:T(8,128)S(1)}, f32[256,2,8]{0,2,1:T(8,128)S(1)}) fusion(f32[2,256,256,8]{2,1,3,0:T(8,128)S(1)} %get-tuple-element.58, f32[256,2,8]{0,2,1:T(8,128)S(1)} %get-tuple-element.16, pred[256,256]{0,1:T(8,128)(4,1)S(1)} %get-tuple-element.46, f32[256,2,8]{0,2,1:T(8,128)S(1)} %get-tuple-element.15, ...), kind=kLoop, calls=%fused_computation.24 | loop fusion | flops 8380416 | bytes 8585216 | tf_op jit(solution)/shard_map/reduce_sum | solution.py:54
  111.4 1.1 fusion.30
  112.6 1.0 copy-done.4
  113.6 1.4 %fusion.32 = f32[2,128,256,8]{2,1,3,0:T(8,128)S(1)} fusion(bf16[256,2,128,1]{0,2,3,1:T(8,128)(2,1)S(1)} %bitcast.251, f32[2,256,256,8]{2,1,3,0:T(8,128)S(1)} %copy-done.4, f32[256,2,8]{0,2,1:T(8,128)S(1)} %get-tuple-element.17, pred[256,256]{0,1:T(8,128)(4,1)S(1)} %get-tuple-element.45), kind=kOutput, calls=%fused_computation.44 | convolution fusion | flops 272629760 | bytes 6504448 | tf_op jit(solution)/shard_map/qcgk,kcd->qcgd/dot_general | solution.py:56
  115.0 0.1 copy-done.3
  115.1 2.0 %fusion.4 = (f32[256,2,8]{0,2,1:T(8,128)S(1)}, f32[256,2,8]{0,2,1:T(8,128)S(1)}) fusion(f32[2,256,256,8]{2,1,3,0:T(8,128)S(1)} %copy-done.3, f32[256,2,8]{0,2,1:T(8,128)S(1)} %get-tuple-element.18, pred[256,256]{0,1:T(8,128)(4,1)S(1)} %get-tuple-element.44, f32[256,2,8]{0,2,1:T(8,128)S(1)} %get-tuple-element.17, f32[2,256,256,8]{2,1,3,0:T(8,128)S(1)} %copy-done.4, ...), kind=kLoop, calls=%fused_computation.20 | loop fusion | flops 8380416 | bytes 8585216 | tf_op jit(solution)/shard_map/reduce_sum | solution.py:54
  117.2 1.1 fusion.34
  118.3 1.1 copy-done.1
  119.4 2.0 %fusion = (f32[256,2,8]{0,2,1:T(8,128)S(1)}, f32[256,2,8]{0,2,1:T(8,128)S(1)}) fusion(f32[2,256,256,8]{2,1,3,0:T(8,128)S(1)} %copy-done.1, f32[256,2,8]{0,2,1:T(8,128)S(1)} %get-tuple-element.63, pred[256,256]{0,1:T(8,128)(4,1)S(1)} %get-tuple-element.50, f32[256,2,8]{0,2,1:T(8,128)S(1)} %get-tuple-element.19, f32[2,256,256,8]{2,1,3,0:T(8,128)S(1)} %copy-done.2, ...), kind=kLoop, calls=%fused_computation.16 | loop fusion | flops 8380416 | bytes 8585216 | tf_op jit(solution)/shard_map/reduce_sum | solution.py:54
  121.4 1.1 fusion.36
  122.6 1.1 fusion.26
  123.7 2.0 %fusion.12 = (f32[256,2,8]{0,2,1:T(8,128)S(1)}, f32[256,2,8]{0,2,1:T(8,128)S(1)}) fusion(f32[2,256,256,8]{2,1,3,0:T(8,128)S(1)} %get-tuple-element.54, f32[256,2,8]{0,2,1:T(8,128)S(1)} %get-tuple-element.14, pred[256,256]{0,1:T(8,128)(4,1)S(1)} %get-tuple-element.48, f32[256,2,8]{0,2,1:T(8,128)S(1)} %get-tuple-element.13, ...), kind=kLoop, calls=%fused_computation.28 | loop fusion | flops 8380416 | bytes 8585216 | tf_op jit(solution)/shard_map/reduce_sum | solution.py:54
  125.8 2.5 %fusion.41 = bf16[256,2,8,128]{0,3,2,1:T(8,128)(2,1)S(1)} fusion(f32[2,128,256,8]{2,1,3,0:T(8,128)S(1)} %fusion.26, f32[2,128,256,8]{2,1,3,0:T(8,128)S(1)} %fusion.28, f32[2,128,256,8]{2,1,3,0:T(8,128)S(1)} %fusion.30, f32[2,128,256,8]{2,1,3,0:T(8,128)S(1)} %fusion.32, f32[2,128,256,8]{2,1,3,0:T(8,128)S(1)} %fusion.34, f32[2,128,256,8]{2,1,3,0:T(8,128)S(1)} %fusion.36, ...), kind=kOutput, calls=%fused_computation.50 | convolution fusion | flops 281542656 | bytes 20283392 | tf_op jit(solution)/shard_map/qcgk,kcd->qcgd/dot_general | solution.py:56
  128.3 1.4 %copy.144 = bf16[256,2048]{1,0:T(8,128)(2,1)} copy(bf16[256,2048]{0,1:T(8,128)(2,1)S(1)} %bitcast.248) | data formatting | bytes 2097152 | tf_op jit(solution)/shard_map/convert_element_type | solution.py:78
  (27 shorter events, 0.2 us)
Async XLA Ops:
  0.0 24.7 %copy-start.13 = (s32[2048]{0:T(1024)S(1)}, s32[2048]{0:T(1024)}, u32[]{:S(2)}) copy-start(s32[2048]{0:T(1024)} %param.7) | copy-start | bytes 24580
  1.6 7.5 %all-to-all-start = ((bf16[64,4,256]{2,0,1:T(8,128)(2,1)}), bf16[64,4,256]{2,0,1:T(8,128)(2,1)S(1)}, u32[]{:S(2)}, u32[]{:S(2)}) async-start(bf16[64,4,256]{2,0,1:T(8,128)(2,1)} %bitcast.233), calls=%async_computation | async-start | bytes 262144 | tf_op jit(solution)/shard_map/all_to_all | solution.py:21
  9.1 7.9 %all-to-all-start.2 = ((bf16[64,4,256]{2,0,1:T(8,128)(2,1)}), bf16[64,4,256]{2,0,1:T(8,128)(2,1)S(1)}, u32[]{:S(2)}, u32[]{:S(2)}) async-start(bf16[64,4,256]{2,0,1:T(8,128)(2,1)} %bitcast.232), calls=%async_computation.2 | async-start | bytes 262144 | tf_op jit(solution)/shard_map/all_to_all | solution.py:22
  17.0 18.8 %all-to-all-start.1 = ((bf16[64,4,2048]{2,0,1:T(8,128)(2,1)}), bf16[64,4,2048]{2,0,1:T(8,128)(2,1)S(1)}, u32[]{:S(2)}, u32[]{:S(2)}) async-start(bf16[64,4,2048]{2,0,1:T(8,128)(2,1)} %bitcast.231), calls=%async_computation.1 | async-start | bytes 2097152 | tf_op jit(solution)/shard_map/all_to_all | solution.py:20
  21.6 10.6 %collective-permute-start = (bf16[1,2,256,256]{3,2,1,0:T(8,128)(2,1)S(1)}, bf16[1,2,256,256]{3,2,1,0:T(8,128)(2,1)S(1)}, u32[]{:S(2)}, u32[]{:S(2)}) collective-permute-start(bf16[1,2,256,256]{3,2,1,0:T(8,128)(2,1)S(1)} %maximum_bitcast_fusion), channel_id=1, source_target_pairs={{0,4},{4,8},{8,12},{12,16},{16,20},{20,24},{24,28},{1,5},{5,9},{9,... | collective-permute-start | bytes 786440 | tf_op jit(solution)/shard_map/ppermute | solution.py:15
  34.5 14.7 %collective-permute-start.1 = (bf16[2,2,256,256]{3,2,1,0:T(8,128)(2,1)}, bf16[2,2,256,256]{3,2,1,0:T(8,128)(2,1)S(1)}, u32[]{:S(2)}, u32[]{:S(2)}) collective-permute-start(bf16[2,2,256,256]{3,2,1,0:T(8,128)(2,1)} %pad_maximum_fusion.1), channel_id=1, source_target_pairs={{0,8},{4,12},{8,16},{12,20},{16,24},{20,28},{1,9},{5,13},{9,17},{1... | collective-permute-start | bytes 1572872 | tf_op jit(solution)/shard_map/ppermute | solution.py:15
  37.9 12.4 %copy-start = (f32[2,256,256,8]{2,1,3,0:T(8,128)}, f32[2,256,256,8]{2,1,3,0:T(8,128)S(1)}, u32[]{:S(2)}) copy-start(f32[2,256,256,8]{2,1,3,0:T(8,128)S(1)} %get-tuple-element.64) | copy-start | bytes 12582916
  37.9 13.9 %copy-start.9 = (bf16[1,1,256,256]{2,3,1,0:T(8,128)(2,1)S(1)}, bf16[1,1,256,256]{2,3,1,0:T(8,128)(2,1)}, u32[]{:S(2)}) copy-start(bf16[1,1,256,256]{2,3,1,0:T(8,128)(2,1)} %copy.109) | copy-start | bytes 393220
  50.3 50.4 %collective-permute-start.2 = (bf16[4,2,256,256]{3,2,1,0:T(8,128)(2,1)}, bf16[4,2,256,256]{3,2,1,0:T(8,128)(2,1)S(1)}, u32[]{:S(2)}, u32[]{:S(2)}) collective-permute-start(bf16[4,2,256,256]{3,2,1,0:T(8,128)(2,1)} %pad_maximum_fusion), channel_id=1, source_target_pairs={{0,16},{4,20},{8,24},{12,28},{1,17},{5,21},{9,25},{13,29},{2,18},{... | collective-permute-start | bytes 3145736 | tf_op jit(solution)/shard_map/ppermute | solution.py:15
  101.5 3.7 %copy-start.6 = (pred[256,256]{0,1:T(8,128)(4,1)S(1)}, pred[256,256]{0,1:T(8,128)(4,1)}, u32[]{:S(2)}) copy-start(pred[256,256]{0,1:T(8,128)(4,1)} %get-tuple-element.47) | copy-start | bytes 196612
  105.2 2.0 %copy-start.7 = (pred[256,256]{0,1:T(8,128)(4,1)S(1)}, pred[256,256]{0,1:T(8,128)(4,1)}, u32[]{:S(2)}) copy-start(pred[256,256]{0,1:T(8,128)(4,1)} %get-tuple-element.49) | copy-start | bytes 196612
  106.2 2.0 %copy-start.10 = (f32[256,2,8]{0,2,1:T(8,128)S(1)}, f32[256,2,8]{0,2,1:T(8,128)}, u32[]{:S(2)}) copy-start(f32[256,2,8]{0,2,1:T(8,128)} %get-tuple-element.65) | copy-start | bytes 49156
  106.2 2.0 %copy-start.11 = (f32[256,2,8]{0,2,1:T(8,128)S(1)}, f32[256,2,8]{0,2,1:T(8,128)}, u32[]{:S(2)}) copy-start(f32[256,2,8]{0,2,1:T(8,128)} %get-tuple-element.61) | copy-start | bytes 49156
  106.2 2.0 %copy-start.12 = (f32[256,2,8]{0,2,1:T(8,128)S(1)}, f32[256,2,8]{0,2,1:T(8,128)}, u32[]{:S(2)}) copy-start(f32[256,2,8]{0,2,1:T(8,128)} %get-tuple-element.59) | copy-start | bytes 49156
  111.4 2.2 %copy-start.4 = (f32[2,256,256,8]{2,1,3,0:T(8,128)S(1)}, f32[2,256,256,8]{2,1,3,0:T(8,128)}, u32[]{:S(2)}) copy-start(f32[2,256,256,8]{2,1,3,0:T(8,128)} %get-tuple-element.60) | copy-start | bytes 12582916
  112.6 2.5 %copy-start.3 = (f32[2,256,256,8]{2,1,3,0:T(8,128)S(1)}, f32[2,256,256,8]{2,1,3,0:T(8,128)}, u32[]{:S(2)}) copy-start(f32[2,256,256,8]{2,1,3,0:T(8,128)} %get-tuple-element.62) | copy-start | bytes 12582916
  115.1 3.2 %copy-start.2 = (f32[2,256,256,8]{2,1,3,0:T(8,128)S(1)}, f32[2,256,256,8]{2,1,3,0:T(8,128)}, u32[]{:S(2)}) copy-start(f32[2,256,256,8]{2,1,3,0:T(8,128)} %get-tuple-element.66) | copy-start | bytes 12582916
  117.2 2.2 %copy-start.1 = (f32[2,256,256,8]{2,1,3,0:T(8,128)S(1)}, f32[2,256,256,8]{2,1,3,0:T(8,128)}, u32[]{:S(2)}) copy-start(f32[2,256,256,8]{2,1,3,0:T(8,128)} %copy-done) | copy-start | bytes 12582916
  119.4 2.0 %copy-start.8 = (bf16[1,1,256,256]{2,3,1,0:T(8,128)(2,1)S(1)}, bf16[1,1,256,256]{2,3,1,0:T(8,128)(2,1)}, u32[]{:S(2)}) copy-start(bf16[1,1,256,256]{2,3,1,0:T(8,128)(2,1)} %copy.112) | copy-start | bytes 393220
  123.7 2.1 %copy-start.5 = (f32[2,256,8,128]{1,3,2,0:T(8,128)S(1)}, f32[2,256,8,128]{1,3,2,0:T(8,128)}, u32[]{:S(2)}) copy-start(f32[2,256,8,128]{1,3,2,0:T(8,128)} %fusion.38) | copy-start | bytes 6291460
where the time goes:
time: 130 us
  waiting for transfers between devices  52.2 us (40%)
  matrix products  29.5 us (23%)
  starting transfers between devices  18.7 us (14%)
  local copies, waits for them, and re-layouts  17.7 us (14%)
  other arithmetic  11.2 us (9%)
    ppermute x3, waiting for transfers between devices, from_behind(): return lax.ppermute(array, axis, pairs)  48.9 us
    dot_general x8, matrix products, absorb(): jnp.einsum('qcgd,kcd->qcgk', query_heads, key_block, preferred_element_ty...  16.3 us
    dot_general x8, matrix products, absorb(): jnp.einsum('qcgk,kcd->qcgd', rounded, value_block, preferred_element_type...  13.2 us
    reduce_sum x4, other arithmetic, absorb(): weight_sum = weight_sum * rescale + jnp.sum(weights, axis=-1)  8.14 us
    ppermute x3, starting transfers between devices, from_behind(): return lax.ppermute(array, axis, pairs)  5.86 us
    slice x10, local copies, waits for them, and re-layouts, absorb(): value_block = key_pair[1].reshape(shard_rows, head_count, HD)  4.61 us
    all_to_all x1, starting transfers between devices, body(): lax.all_to_all(queries, 'head', split_axis=1, concat_axis=0, tiled=True)  4.53 us
    all_to_all x1, starting transfers between devices, body(): lax.all_to_all(values, 'head', split_axis=1, concat_axis=0, tiled=True)  4.33 us
  transfers between devices with their start and end apart: 6, of which 5 were waited for; matrix products, arithmetic and copies ran while one was open for 21% of the time, Pallas kernels for 0%

commit v1 on v0

--- a/solution.py
+++ b/solution.py
@@ -7,6 +7,29 @@
 KVH = 8
 HD = 128
 REACH = 7
+
+
+def in_blocks(shard, dim, size):
+    shape = shard.shape
+    parts = shard.reshape(*shape[:dim], size, shape[dim] // size, *shape[dim + 1 :])
+    return jnp.moveaxis(parts, dim, 0)
+
+
+def in_order(blocks, dim):
+    lengths = list(blocks.shape[1:])
+    lengths[dim] *= blocks.shape[0]
+    return jnp.moveaxis(blocks, 0, dim).reshape(lengths)
+
+
+def swapped_with_each(shard, axis, split_dim, concat_dim):
+    peers, index = (lax.axis_size(axis), lax.axis_index(axis))
+    tiles = in_blocks(shard, split_dim, peers)
+    outs = [tiles[index]]
+    for step in range(1, peers):
+        sent = tiles[index ^ step]
+        outs.append(lax.ppermute(sent, axis, [(i, i ^ step) for i in range(peers)]))
+    tiles = jnp.stack(outs)[index ^ jnp.arange(peers)]
+    return in_order(tiles, concat_dim)
 
 
 def from_behind(array, axis, by):
@@ -19,7 +42,7 @@
     local_queries, local_keys, local_values = (
         lax.all_to_all(queries, "head", split_axis=1, concat_axis=0, tiled=True),
         lax.all_to_all(keys, "head", split_axis=1, concat_axis=0, tiled=True),
-        lax.all_to_all(values, "head", split_axis=1, concat_axis=0, tiled=True),
+        swapped_with_each(values, "head", 1, 0),
     )
     shard_rows = local_queries.shape[0]
     head_count = local_keys.shape[1] // HD

time: 130 us -> 125 us (0.962)
  starting transfers between devices: 18.7 us -> 15.9 us
  waiting for transfers between devices: 52.2 us -> 49.7 us
    all_to_all x1 -> x0, starting transfers between devices: 4.33 us -> none  [body(): lax.all_to_all(values, 'head', split_axis=1, concat_axis=0, tiled=True)]
    ppermute x0 -> x3, starting transfers between devices: none -> 2.21 us  [swapped_with_each(): outs.append(lax.ppermute(sent, axis, [(i, i ^ step) for i in range(peers)]))]
    all_to_all x1, waiting for transfers between devices: 2.02 us -> 0.01 us  [body(): lax.all_to_all(keys, 'head', split_axis=1, concat_axis=0, tiled=True)]
    all_to_all x1 -> x0, local copies, waits for them, and re-layouts: 1.55 us -> none  [body(): lax.all_to_all(values, 'head', split_axis=1, concat_axis=0, tiled=True)]
  transfers between devices with their start and end apart: 6 -> 8, of which waited for: 5 -> 4; matrix products, arithmetic and copies ran while one was open for 21% -> 22% of each run, Pallas kernels for 0% -> 0%
where the time goes in v1:
time: 125 us
  waiting for transfers between devices  49.7 us (40%)
  matrix products  29.5 us (24%)
  local copies, waits for them, and re-layouts  18 us (14%)
  starting transfers between devices  15.9 us (13%)
  other arithmetic  11.2 us (9%)
    ppermute x3, waiting for transfers between devices, from_behind(): return lax.ppermute(array, axis, pairs)  49 us
    dot_general x8, matrix products, absorb(): jnp.einsum('qcgd,kcd->qcgk', query_heads, key_block, preferred_element_ty...  16.3 us
    dot_general x8, matrix products, absorb(): jnp.einsum('qcgk,kcd->qcgd', rounded, value_block, preferred_element_type...  13.2 us
    reduce_sum x4, other arithmetic, absorb(): weight_sum = weight_sum * rescale + jnp.sum(weights, axis=-1)  8.14 us
    ppermute x3, starting transfers between devices, from_behind(): return lax.ppermute(array, axis, pairs)  5.86 us
    slice x10, local copies, waits for them, and re-layouts, absorb(): value_block = key_pair[1].reshape(shard_rows, head_count, HD)  4.61 us
    all_to_all x1, starting transfers between devices, body(): lax.all_to_all(keys, 'head', split_axis=1, concat_axis=0, tiled=True)  3.96 us
    all_to_all x1, starting transfers between devices, body(): lax.all_to_all(queries, 'head', split_axis=1, concat_axis=0, tiled=True)  3.89 us
  transfers between devices with their start and end apart: 8, of which 4 were waited for; matrix products, arithmetic and copies ran while one was open for 22% of the time, Pallas kernels for 0%

profile of v1, /device:TPU:25, one launch (start us, length us, event | category | flops | bytes accessed | tf_op | source)
XLA Modules:
  0.0 124.8 jit_solution(5781248626213043250)
XLA Ops:
  0.0 1.6 %copy.235 = bf16[8,4,8,256]{3,2,0,1:T(8,128)(2,1)} copy(bf16[8,4,8,256]{3,2,1,0:T(8,128)(2,1)} %bitcast.274) | data formatting | bytes 262144 | tf_op jit(solution)/shard_map/all_to_all | solution.py:44
  1.6 4.0 %all-to-all-start = ((bf16[64,4,256]{2,0,1:T(8,128)(2,1)}), bf16[64,4,256]{2,0,1:T(8,128)(2,1)S(1)}, u32[]{:S(2)}, u32[]{:S(2)}) async-start(bf16[64,4,256]{2,0,1:T(8,128)(2,1)} %bitcast.240), calls=%async_computation | async-start | bytes 262144 | tf_op jit(solution)/shard_map/all_to_all | solution.py:44
  5.5 1.0 reshape.465
  6.5 0.3 constant_dynamic-slice_fusion.3
  6.8 0.1 collective-permute-start
  7.0 1.7 %collective-permute-start.1 = (bf16[64,256]{1,0:T(8,128)(2,1)S(1)}, bf16[64,256]{1,0:T(8,128)(2,1)S(1)}, u32[]{:S(2)}, u32[]{:S(2)}) collective-permute-start(bf16[64,256]{1,0:T(8,128)(2,1)S(1)} %bitcast.278), channel_id=1, source_target_pairs={{0,2},{1,3},{2,0},{3,1},{4,6},{5,7},{6,4},{7,5},{8,10},{9,11},{10,... | collective-permute-start | bytes 98312 | tf_op jit(solution)/shard_map/ppermute | solution.py:30
  8.7 0.4 collective-permute-start.2
  9.1 2.3 %copy.234 = bf16[8,4,8,2048]{3,2,0,1:T(8,128)(2,1)} copy(bf16[8,4,8,2048]{3,2,1,0:T(8,128)(2,1)} %bitcast.257) | data formatting | bytes 2097152 | tf_op jit(solution)/shard_map/all_to_all | solution.py:43
  11.4 0.7 collective-permute-done.2
  12.1 0.6 gather_fusion
  12.7 3.9 %all-to-all-start.1 = ((bf16[64,4,2048]{2,0,1:T(8,128)(2,1)}), bf16[64,4,2048]{2,0,1:T(8,128)(2,1)S(1)}, u32[]{:S(2)}, u32[]{:S(2)}) async-start(bf16[64,4,2048]{2,0,1:T(8,128)(2,1)} %bitcast.239), calls=%async_computation.1 | async-start | bytes 2097152 | tf_op jit(solution)/shard_map/all_to_all | solution.py:43
  16.6 3.1 %collective-permute-start.3 = (bf16[1,2,256,256]{3,2,1,0:T(8,128)(2,1)S(1)}, bf16[1,2,256,256]{3,2,1,0:T(8,128)(2,1)S(1)}, u32[]{:S(2)}, u32[]{:S(2)}) collective-permute-start(bf16[1,2,256,256]{3,2,1,0:T(8,128)(2,1)S(1)} %maximum_bitcast_fusion), channel_id=1, source_target_pairs={{0,4},{4,8},{8,12},{12,16},{16,20},{20,24},{24,28},{1,5},{5,9},{9,... | collective-permute-start | bytes 786440 | tf_op jit(solution)/shard_map/ppermute | solution.py:38
  19.7 0.1 pad_dynamic-slice_fusion.6
  19.9 1.0 broadcast_compare_fusion.6
  20.9 0.7 reshape_squeeze_stack_reshape.3
  21.6 0.7 reshape_squeeze_stack.3
  22.3 4.9 %collective-permute-done.3 = bf16[1,2,256,256]{3,2,1,0:T(8,128)(2,1)S(1)} collective-permute-done((bf16[1,2,256,256]{3,2,1,0:T(8,128)(2,1)S(1)}, bf16[1,2,256,256]{3,2,1,0:T(8,128)(2,1)S(1)}, u32[]{:S(2)}, u32[]{:S(2)}) %collective-permute-start.3) | collective-permute-done | bytes 262176 | tf_op jit(solution)/shard_map/ppermute | solution.py:38
  27.2 0.7 copy.108
  28.0 0.8 copy.105
  28.7 0.8 pad_maximum_fusion.1
  29.6 1.3 %collective-permute-start.4 = (bf16[2,2,256,256]{3,2,1,0:T(8,128)(2,1)}, bf16[2,2,256,256]{3,2,1,0:T(8,128)(2,1)S(1)}, u32[]{:S(2)}, u32[]{:S(2)}) collective-permute-start(bf16[2,2,256,256]{3,2,1,0:T(8,128)(2,1)} %pad_maximum_fusion.1), channel_id=1, source_target_pairs={{0,8},{4,12},{8,16},{12,20},{16,24},{20,28},{1,9},{5,13},{9,17},{1... | collective-permute-start | bytes 1572872 | tf_op jit(solution)/shard_map/ppermute | solution.py:38
  30.9 0.2 copy.189
  31.1 1.8 %fusion.16 = (f32[256,2,8]{0,2,1:T(8,128)S(1)}, f32[2,256,256,8]{2,1,3,0:T(8,128)S(1)}) fusion(pred[256,256]{0,1:T(8,128)(4,1)S(1)} %get-tuple-element.54, bf16[256,2,8,128]{3,2,1,0:T(8,128)(2,1)S(1)} %bitcast.245, bf16[256,2,128,1]{2,1,0,3:T(2,128)(2,1)} %bitcast.268), kind=kOutput, calls=%fused_computation.33 | convolution fusion | flops 271577088 | bytes 5455872 | tf_op jit(solution)/shard_map/qcgd,kcd->qcgk/dot_general | solution.py:70
  33.0 3.6 %fusion.38 = f32[2,128,256,8]{2,1,3,0:T(8,128)} fusion(f32[2,256,256,8]{2,1,3,0:T(8,128)S(1)} %get-tuple-element.68, f32[256,2,8]{0,2,1:T(8,128)S(1)} %get-tuple-element.67, pred[256,256]{0,1:T(8,128)(4,1)S(1)} %get-tuple-element.54, bf16[256,2,128,1]{2,1,0,3:T(2,128)(2,1)} %bitcast.266), kind=kOutput, calls=%fused_computation.48 | convolution fusion | flops 272629760 | bytes 6504448 | tf_op jit(solution)/shard_map/qcgk,kcd->qcgd/dot_general | solution.py:79
  36.6 7.7 %collective-permute-done.4 = bf16[2,2,256,256]{3,2,1,0:T(8,128)(2,1)S(1)} collective-permute-done((bf16[2,2,256,256]{3,2,1,0:T(8,128)(2,1)}, bf16[2,2,256,256]{3,2,1,0:T(8,128)(2,1)S(1)}, u32[]{:S(2)}, u32[]{:S(2)}) %collective-permute-start.4) | collective-permute-done | bytes 524320 | tf_op jit(solution)/shard_map/ppermute | solution.py:38
  44.3 1.1 pad_maximum_fusion
  45.3 1.5 %collective-permute-start.5 = (bf16[4,2,256,256]{3,2,1,0:T(8,128)(2,1)}, bf16[4,2,256,256]{3,2,1,0:T(8,128)(2,1)S(1)}, u32[]{:S(2)}, u32[]{:S(2)}) collective-permute-start(bf16[4,2,256,256]{3,2,1,0:T(8,128)(2,1)} %pad_maximum_fusion), channel_id=1, source_target_pairs={{0,16},{4,20},{8,24},{12,28},{1,17},{5,21},{9,25},{13,29},{2,18},{... | collective-permute-start | bytes 3145736 | tf_op jit(solution)/shard_map/ppermute | solution.py:38
  46.8 3.5 %fusion.17 = (f32[256,2,8]{0,2,1:T(8,128)}, f32[2,256,256,8]{2,1,3,0:T(8,128)}) fusion(pred[256,256]{0,1:T(8,128)(4,1)S(1)} %get-tuple-element.47, bf16[256,2,128,1]{0,2,3,1:T(8,128)(2,1)S(1)} %bitcast.265, bf16[256,2,8,128]{3,2,1,0:T(8,128)(2,1)S(1)} %bitcast.246), kind=kOutput, calls=%fused_computation.34 | convolution fusion | flops 271577088 | bytes 5455872 | tf_op jit(solution)/shard_map/qcgd,kcd->qcgk/dot_general | solution.py:70
  50.3 0.7 fusion.121
  51.0 0.1 copy.113
  51.1 0.1 copy.118
  51.2 0.1 copy.115
  51.4 1.0 copy.110
  52.4 3.5 %fusion.18 = (f32[256,2,8]{0,2,1:T(8,128)}, f32[2,256,256,8]{2,1,3,0:T(8,128)}) fusion(pred[256,256]{0,1:T(8,128)(4,1)S(1)} %get-tuple-element.48, bf16[256,2,128,1]{0,2,3,1:T(8,128)(2,1)S(1)} %bitcast.272, bf16[256,2,8,128]{3,2,1,0:T(8,128)(2,1)S(1)} %bitcast.247), kind=kOutput, calls=%fused_computation.35 | convolution fusion | flops 271577088 | bytes 5455872 | tf_op jit(solution)/shard_map/qcgd,kcd->qcgk/dot_general | solution.py:70
  55.9 3.5 %fusion.19 = (f32[256,2,8]{0,2,1:T(8,128)}, f32[2,256,256,8]{2,1,3,0:T(8,128)}) fusion(pred[256,256]{0,1:T(8,128)(4,1)S(1)} %get-tuple-element.49, bf16[256,2,128,1]{0,2,3,1:T(8,128)(2,1)S(1)} %bitcast.271, bf16[256,2,8,128]{3,2,1,0:T(8,128)(2,1)S(1)} %bitcast.248), kind=kOutput, calls=%fused_computation.36 | convolution fusion | flops 271577088 | bytes 5455872 | tf_op jit(solution)/shard_map/qcgd,kcd->qcgk/dot_general | solution.py:70
  59.4 36.4 %collective-permute-done.5 = bf16[4,2,256,256]{3,2,1,0:T(8,128)(2,1)S(1)} collective-permute-done((bf16[4,2,256,256]{3,2,1,0:T(8,128)(2,1)}, bf16[4,2,256,256]{3,2,1,0:T(8,128)(2,1)S(1)}, u32[]{:S(2)}, u32[]{:S(2)}) %collective-permute-start.5) | collective-permute-done | bytes 1048608 | tf_op jit(solution)/shard_map/ppermute | solution.py:38
  95.8 0.8 fusion.120
  96.5 0.1 copy.138
  96.6 0.1 copy.135
  96.8 0.1 copy.133
  96.9 0.1 copy.130
  97.0 1.0 copy.128
  98.0 0.1 copy.125
  98.1 1.0 copy.123
  99.1 0.1 copy.120
  99.2 1.0 fusion.20
  100.2 1.0 fusion.21
  101.2 1.0 fusion.22
  102.2 1.0 fusion.23
  103.3 1.1 fusion.28
  104.4 2.0 %fusion.8 = (f32[256,2,8]{0,2,1:T(8,128)S(1)}, f32[256,2,8]{0,2,1:T(8,128)S(1)}) fusion(f32[2,256,256,8]{2,1,3,0:T(8,128)S(1)} %get-tuple-element.62, f32[256,2,8]{0,2,1:T(8,128)S(1)} %get-tuple-element.16, pred[256,256]{0,1:T(8,128)(4,1)S(1)} %get-tuple-element.50, f32[256,2,8]{0,2,1:T(8,128)S(1)} %get-tuple-element.15, ...), kind=kLoop, calls=%fused_computation.25 | loop fusion | flops 8380416 | bytes 8585216 | tf_op jit(solution)/shard_map/reduce_sum | solution.py:77
  106.5 1.1 fusion.30
  107.6 1.0 copy-done.4
  108.7 1.4 %fusion.32 = f32[2,128,256,8]{2,1,3,0:T(8,128)S(1)} fusion(bf16[256,2,128,1]{0,2,3,1:T(8,128)(2,1)S(1)} %bitcast.261, f32[2,256,256,8]{2,1,3,0:T(8,128)S(1)} %copy-done.4, f32[256,2,8]{0,2,1:T(8,128)S(1)} %get-tuple-element.17, pred[256,256]{0,1:T(8,128)(4,1)S(1)} %get-tuple-element.49), kind=kOutput, calls=%fused_computation.45 | convolution fusion | flops 272629760 | bytes 6504448 | tf_op jit(solution)/shard_map/qcgk,kcd->qcgd/dot_general | solution.py:79
  110.0 0.1 copy-done.3
  110.2 2.0 %fusion.4 = (f32[256,2,8]{0,2,1:T(8,128)S(1)}, f32[256,2,8]{0,2,1:T(8,128)S(1)}) fusion(f32[2,256,256,8]{2,1,3,0:T(8,128)S(1)} %copy-done.3, f32[256,2,8]{0,2,1:T(8,128)S(1)} %get-tuple-element.18, pred[256,256]{0,1:T(8,128)(4,1)S(1)} %get-tuple-element.48, f32[256,2,8]{0,2,1:T(8,128)S(1)} %get-tuple-element.17, f32[2,256,256,8]{2,1,3,0:T(8,128)S(1)} %copy-done.4, ...), kind=kLoop, calls=%fused_computation.21 | loop fusion | flops 8380416 | bytes 8585216 | tf_op jit(solution)/shard_map/reduce_sum | solution.py:77
  112.2 1.1 fusion.34
  113.4 1.0 copy-done.1
  114.4 2.0 %fusion = (f32[256,2,8]{0,2,1:T(8,128)S(1)}, f32[256,2,8]{0,2,1:T(8,128)S(1)}) fusion(f32[2,256,256,8]{2,1,3,0:T(8,128)S(1)} %copy-done.1, f32[256,2,8]{0,2,1:T(8,128)S(1)} %get-tuple-element.67, pred[256,256]{0,1:T(8,128)(4,1)S(1)} %get-tuple-element.54, f32[256,2,8]{0,2,1:T(8,128)S(1)} %get-tuple-element.19, f32[2,256,256,8]{2,1,3,0:T(8,128)S(1)} %copy-done.2, ...), kind=kLoop, calls=%fused_computation.17 | loop fusion | flops 8380416 | bytes 8585216 | tf_op jit(solution)/shard_map/reduce_sum | solution.py:77
  116.5 1.1 fusion.36
  117.6 1.1 fusion.26
  118.8 2.0 %fusion.12 = (f32[256,2,8]{0,2,1:T(8,128)S(1)}, f32[256,2,8]{0,2,1:T(8,128)S(1)}) fusion(f32[2,256,256,8]{2,1,3,0:T(8,128)S(1)} %get-tuple-element.58, f32[256,2,8]{0,2,1:T(8,128)S(1)} %get-tuple-element.14, pred[256,256]{0,1:T(8,128)(4,1)S(1)} %get-tuple-element.52, f32[256,2,8]{0,2,1:T(8,128)S(1)} %get-tuple-element.13, ...), kind=kLoop, calls=%fused_computation.29 | loop fusion | flops 8380416 | bytes 8585216 | tf_op jit(solution)/shard_map/reduce_sum | solution.py:77
  120.9 2.5 %fusion.41 = bf16[256,2,8,128]{0,3,2,1:T(8,128)(2,1)S(1)} fusion(f32[2,128,256,8]{2,1,3,0:T(8,128)S(1)} %fusion.26, f32[2,128,256,8]{2,1,3,0:T(8,128)S(1)} %fusion.28, f32[2,128,256,8]{2,1,3,0:T(8,128)S(1)} %fusion.30, f32[2,128,256,8]{2,1,3,0:T(8,128)S(1)} %fusion.32, f32[2,128,256,8]{2,1,3,0:T(8,128)S(1)} %fusion.34, f32[2,128,256,8]{2,1,3,0:T(8,128)S(1)} %fusion.36, ...), kind=kOutput, calls=%fused_computation.51 | convolution fusion | flops 281542656 | bytes 20283392 | tf_op jit(solution)/shard_map/qcgk,kcd->qcgd/dot_general | solution.py:79
  123.4 1.4 %copy.140 = bf16[256,2048]{1,0:T(8,128)(2,1)} copy(bf16[256,2048]{0,1:T(8,128)(2,1)S(1)} %bitcast.258) | data formatting | bytes 2097152 | tf_op jit(solution)/shard_map/convert_element_type | solution.py:101
  (40 shorter events, 0.2 us)
Async XLA Ops:
  0.0 19.7 %copy-start.13 = (s32[2048]{0:T(1024)S(1)}, s32[2048]{0:T(1024)}, u32[]{:S(2)}) copy-start(s32[2048]{0:T(1024)} %param.7) | copy-start | bytes 24580
  1.6 11.1 %all-to-all-start = ((bf16[64,4,256]{2,0,1:T(8,128)(2,1)}), bf16[64,4,256]{2,0,1:T(8,128)(2,1)S(1)}, u32[]{:S(2)}, u32[]{:S(2)}) async-start(bf16[64,4,256]{2,0,1:T(8,128)(2,1)} %bitcast.240), calls=%async_computation | async-start | bytes 262144 | tf_op jit(solution)/shard_map/all_to_all | solution.py:44
  6.8 4.6 %collective-permute-start = (bf16[64,256]{1,0:T(8,128)(2,1)S(1)}, bf16[64,256]{1,0:T(8,128)(2,1)S(1)}, u32[]{:S(2)}, u32[]{:S(2)}) collective-permute-start(bf16[64,256]{1,0:T(8,128)(2,1)S(1)} %bitcast.277), channel_id=1, source_target_pairs={{0,1},{1,0},{2,3},{3,2},{4,5},{5,4},{6,7},{7,6},{8,9},{9,8},{10,11... | collective-permute-start | bytes 98312 | tf_op jit(solution)/shard_map/ppermute | solution.py:30
  7.0 4.4 %collective-permute-start.1 = (bf16[64,256]{1,0:T(8,128)(2,1)S(1)}, bf16[64,256]{1,0:T(8,128)(2,1)S(1)}, u32[]{:S(2)}, u32[]{:S(2)}) collective-permute-start(bf16[64,256]{1,0:T(8,128)(2,1)S(1)} %bitcast.278), channel_id=1, source_target_pairs={{0,2},{1,3},{2,0},{3,1},{4,6},{5,7},{6,4},{7,5},{8,10},{9,11},{10,... | collective-permute-start | bytes 98312 | tf_op jit(solution)/shard_map/ppermute | solution.py:30
  8.7 3.4 %collective-permute-start.2 = (bf16[64,256]{1,0:T(8,128)(2,1)S(1)}, bf16[64,256]{1,0:T(8,128)(2,1)S(1)}, u32[]{:S(2)}, u32[]{:S(2)}) collective-permute-start(bf16[64,256]{1,0:T(8,128)(2,1)S(1)} %bitcast.279), channel_id=1, source_target_pairs={{0,3},{1,2},{2,1},{3,0},{4,7},{5,6},{6,5},{7,4},{8,11},{9,10},{10,... | collective-permute-start | bytes 98312 | tf_op jit(solution)/shard_map/ppermute | solution.py:30
  12.7 18.2 %all-to-all-start.1 = ((bf16[64,4,2048]{2,0,1:T(8,128)(2,1)}), bf16[64,4,2048]{2,0,1:T(8,128)(2,1)S(1)}, u32[]{:S(2)}, u32[]{:S(2)}) async-start(bf16[64,4,2048]{2,0,1:T(8,128)(2,1)} %bitcast.239), calls=%async_computation.1 | async-start | bytes 2097152 | tf_op jit(solution)/shard_map/all_to_all | solution.py:43
  16.6 10.6 %collective-permute-start.3 = (bf16[1,2,256,256]{3,2,1,0:T(8,128)(2,1)S(1)}, bf16[1,2,256,256]{3,2,1,0:T(8,128)(2,1)S(1)}, u32[]{:S(2)}, u32[]{:S(2)}) collective-permute-start(bf16[1,2,256,256]{3,2,1,0:T(8,128)(2,1)S(1)} %maximum_bitcast_fusion), channel_id=1, source_target_pairs={{0,4},{4,8},{8,12},{12,16},{16,20},{20,24},{24,28},{1,5},{5,9},{9,... | collective-permute-start | bytes 786440 | tf_op jit(solution)/shard_map/ppermute | solution.py:38
  29.6 14.7 %collective-permute-start.4 = (bf16[2,2,256,256]{3,2,1,0:T(8,128)(2,1)}, bf16[2,2,256,256]{3,2,1,0:T(8,128)(2,1)S(1)}, u32[]{:S(2)}, u32[]{:S(2)}) collective-permute-start(bf16[2,2,256,256]{3,2,1,0:T(8,128)(2,1)} %pad_maximum_fusion.1), channel_id=1, source_target_pairs={{0,8},{4,12},{8,16},{12,20},{16,24},{20,28},{1,9},{5,13},{9,17},{1... | collective-permute-start | bytes 1572872 | tf_op jit(solution)/shard_map/ppermute | solution.py:38
  32.9 12.4 %copy-start = (f32[2,256,256,8]{2,1,3,0:T(8,128)}, f32[2,256,256,8]{2,1,3,0:T(8,128)S(1)}, u32[]{:S(2)}) copy-start(f32[2,256,256,8]{2,1,3,0:T(8,128)S(1)} %get-tuple-element.68) | copy-start | bytes 12582916
  32.9 13.9 %copy-start.9 = (bf16[1,1,256,256]{2,3,1,0:T(8,128)(2,1)S(1)}, bf16[1,1,256,256]{2,3,1,0:T(8,128)(2,1)}, u32[]{:S(2)}) copy-start(bf16[1,1,256,256]{2,3,1,0:T(8,128)(2,1)} %copy.105) | copy-start | bytes 393220
  45.3 50.4 %collective-permute-start.5 = (bf16[4,2,256,256]{3,2,1,0:T(8,128)(2,1)}, bf16[4,2,256,256]{3,2,1,0:T(8,128)(2,1)S(1)}, u32[]{:S(2)}, u32[]{:S(2)}) collective-permute-start(bf16[4,2,256,256]{3,2,1,0:T(8,128)(2,1)} %pad_maximum_fusion), channel_id=1, source_target_pairs={{0,16},{4,20},{8,24},{12,28},{1,17},{5,21},{9,25},{13,29},{2,18},{... | collective-permute-start | bytes 3145736 | tf_op jit(solution)/shard_map/ppermute | solution.py:38
  96.5 3.7 %copy-start.6 = (pred[256,256]{0,1:T(8,128)(4,1)S(1)}, pred[256,256]{0,1:T(8,128)(4,1)}, u32[]{:S(2)}) copy-start(pred[256,256]{0,1:T(8,128)(4,1)} %get-tuple-element.51) | copy-start | bytes 196612
  100.2 2.0 %copy-start.7 = (pred[256,256]{0,1:T(8,128)(4,1)S(1)}, pred[256,256]{0,1:T(8,128)(4,1)}, u32[]{:S(2)}) copy-start(pred[256,256]{0,1:T(8,128)(4,1)} %get-tuple-element.53) | copy-start | bytes 196612
  101.2 2.0 %copy-start.10 = (f32[256,2,8]{0,2,1:T(8,128)S(1)}, f32[256,2,8]{0,2,1:T(8,128)}, u32[]{:S(2)}) copy-start(f32[256,2,8]{0,2,1:T(8,128)} %get-tuple-element.69) | copy-start | bytes 49156
  101.2 2.0 %copy-start.11 = (f32[256,2,8]{0,2,1:T(8,128)S(1)}, f32[256,2,8]{0,2,1:T(8,128)}, u32[]{:S(2)}) copy-start(f32[256,2,8]{0,2,1:T(8,128)} %get-tuple-element.65) | copy-start | bytes 49156
  101.2 2.0 %copy-start.12 = (f32[256,2,8]{0,2,1:T(8,128)S(1)}, f32[256,2,8]{0,2,1:T(8,128)}, u32[]{:S(2)}) copy-start(f32[256,2,8]{0,2,1:T(8,128)} %get-tuple-element.63) | copy-start | bytes 49156
  106.5 2.2 %copy-start.4 = (f32[2,256,256,8]{2,1,3,0:T(8,128)S(1)}, f32[2,256,256,8]{2,1,3,0:T(8,128)}, u32[]{:S(2)}) copy-start(f32[2,256,256,8]{2,1,3,0:T(8,128)} %get-tuple-element.64) | copy-start | bytes 12582916
  107.6 2.5 %copy-start.3 = (f32[2,256,256,8]{2,1,3,0:T(8,128)S(1)}, f32[2,256,256,8]{2,1,3,0:T(8,128)}, u32[]{:S(2)}) copy-start(f32[2,256,256,8]{2,1,3,0:T(8,128)} %get-tuple-element.66) | copy-start | bytes 12582916
  110.2 3.2 %copy-start.2 = (f32[2,256,256,8]{2,1,3,0:T(8,128)S(1)}, f32[2,256,256,8]{2,1,3,0:T(8,128)}, u32[]{:S(2)}) copy-start(f32[2,256,256,8]{2,1,3,0:T(8,128)} %get-tuple-element.70) | copy-start | bytes 12582916
  112.2 2.2 %copy-start.1 = (f32[2,256,256,8]{2,1,3,0:T(8,128)S(1)}, f32[2,256,256,8]{2,1,3,0:T(8,128)}, u32[]{:S(2)}) copy-start(f32[2,256,256,8]{2,1,3,0:T(8,128)} %copy-done) | copy-start | bytes 12582916
  114.4 2.0 %copy-start.8 = (bf16[1,1,256,256]{2,3,1,0:T(8,128)(2,1)S(1)}, bf16[1,1,256,256]{2,3,1,0:T(8,128)(2,1)}, u32[]{:S(2)}) copy-start(bf16[1,1,256,256]{2,3,1,0:T(8,128)(2,1)} %copy.108) | copy-start | bytes 393220
  118.8 2.1 %copy-start.5 = (f32[2,128,256,8]{2,1,3,0:T(8,128)S(1)}, f32[2,128,256,8]{2,1,3,0:T(8,128)}, u32[]{:S(2)}) copy-start(f32[2,128,256,8]{2,1,3,0:T(8,128)} %fusion.38) | copy-start | bytes 6291460
